TPU v7x, 512 devices: a whole 4x8x8 slice. The times are simulated.
512 devices in a mesh: wide: 64 (over y, z), narrow: 8 (over x, core).
Axes of the slice: x: 4, y: 8, z: 8, core: 2. Of those that a mesh axis runs over, the one named last changes fastest.
Arguments:
- cand_ids: int32 [128, 32768], P(None, ('wide', 'narrow')), may hold values from 0 to 59999
- cand_request: int32 [32768], P(('wide', 'narrow')), may hold values from 0 to 7
- tables: bfloat16 [128, 1024, 256], P('wide'), may hold values from -4 to 4
- table_rows: int32 [128], P('wide'), may hold values from 256 to 1024
- width_choice: int32 [128], P('wide'), may hold values from 0 to 3
- projections: bfloat16 [128, 256, 128], P('wide'), may hold values from -0.5 to 0.5
- user_dense: bfloat16 [512, 512], P(('wide', 'narrow')), may hold values from -6 to 6
- user_weight: bfloat16 [512, 1024], replicated, may hold values from -0.25 to 0.25
- cross_down: bfloat16 [2048, 256], P('narrow'), may hold values from -0.125 to 0.125
- cross_up: bfloat16 [256, 2048], P(None, 'narrow'), may hold values from -0.375 to 0.375
- cross_bias: float32 [2048], replicated, may hold values from -3 to 3
- deep_in: bfloat16 [2048, 512], P('narrow'), may hold values from -0.125 to 0.125
- deep_mid: bfloat16 [512, 256], replicated, may hold values from -0.25 to 0.25
- head_cross: float32 [2048], replicated, may hold values from -0.125 to 0.125
- head_deep: float32 [256], replicated, may hold values from -0.375 to 0.375
Outputs:
- crossed: bfloat16 [32768, 2048], P(('wide', 'narrow'))
- scores: float32 [32768], P(('wide', 'narrow'))
All inputs are finite; a program needn't handle non-finite values.
Results may differ from a plain program's by a relative error of at most 0.0072.
Values may be sent and summed in bfloat16 or wider, within the bound.
No kernel may reach another device: no remote copies, remote signals or barrier semaphores. Data moves between devices by JAX's collectives and lax.ppermute only.
A program may use at most 64 MiB of HBM per device.

v0:
```python
import jax
import jax.numpy as jnp
from jax import lax
from jax.sharding import PartitionSpec as P

SLOTS = 8


def per_device(
    cand_ids,
    cand_request,
    tables,
    table_rows,
    width_choice,
    projections,
    user_dense,
    user_weight,
    cross_down,
    cross_up,
    cross_bias,
    deep_in,
    deep_mid,
    head_cross,
    head_deep,
):
    nwide = lax.axis_size("wide")
    tab_dev = tables.shape[0]
    emb_width = tables.shape[2]
    rows_dev = cand_request.shape[0]
    columns = jnp.arange(emb_width, dtype=jnp.int32)

    def width_mask(t):
        width = jnp.left_shift(jnp.int32(32), width_choice[t])
        return columns < width

    projected = [
        jnp.dot(
            jnp.where(width_mask(t)[None, :], tables[t], jnp.zeros((), jnp.bfloat16)),
            projections[t],
            preferred_element_type=jnp.float32,
        ).astype(jnp.bfloat16)
        for t in range(tab_dev)
    ]
    feature_ids = cand_ids.reshape(nwide, tab_dev, rows_dev)
    received = lax.all_to_all(feature_ids, "wide", split_axis=0, concat_axis=0, tiled=True)
    results = []
    for t in range(tab_dev):
        index = jnp.remainder(received[:, t, :], table_rows[t])
        results.append(jnp.take(projected[t], index, axis=0))
    stacked = jnp.stack(results, axis=1)
    pooled = jnp.sum(stacked, axis=1, keepdims=True, dtype=jnp.float32).astype(jnp.bfloat16)
    returned = lax.all_to_all(pooled, "wide", split_axis=0, concat_axis=0, tiled=True)
    owners = jnp.sum(returned, axis=1, dtype=jnp.float32).astype(jnp.bfloat16)
    slots = jnp.sum(
        owners.reshape(nwide // SLOTS, SLOTS, rows_dev, owners.shape[2]), axis=0, dtype=jnp.float32
    ).astype(jnp.bfloat16)
    item = slots.transpose(1, 0, 2).reshape(rows_dev, SLOTS * owners.shape[2])
    mine = jax.nn.silu(jnp.dot(user_dense, user_weight, preferred_element_type=jnp.float32)).astype(
        jnp.bfloat16
    )
    users = lax.all_gather(mine, "narrow", axis=0, tiled=True)
    req_count = users.shape[0]
    selector = (cand_request[:, None] == jnp.arange(req_count, dtype=jnp.int32)[None, :]).astype(
        jnp.bfloat16
    )
    user_part = jnp.dot(selector, users, preferred_element_type=jnp.float32).astype(jnp.bfloat16)
    x0 = jnp.concatenate([user_part, item], axis=1)
    low_sum = jnp.dot(
        x0,
        lax.all_gather(cross_down, "narrow", axis=0, tiled=True),
        preferred_element_type=jnp.float32,
    )
    deep_sum = jnp.dot(
        x0,
        lax.all_gather(deep_in, "narrow", axis=0, tiled=True),
        preferred_element_type=jnp.float32,
    )
    low = low_sum.astype(jnp.bfloat16)
    deep = jax.nn.relu(deep_sum).astype(jnp.bfloat16)
    upward = jnp.dot(
        low,
        lax.all_gather(cross_up, "narrow", axis=1, tiled=True),
        preferred_element_type=jnp.float32,
    )
    base = x0.astype(jnp.float32)
    crossed = (base * (upward + cross_bias) + base).astype(jnp.bfloat16)
    hidden = jax.nn.relu(jnp.dot(deep, deep_mid, preferred_element_type=jnp.float32))
    scores = jnp.dot(crossed.astype(jnp.float32), head_cross, precision=lax.Precision.HIGHEST)
    scores = scores + jnp.dot(hidden, head_deep, precision=lax.Precision.HIGHEST)
    return (crossed, scores)


def solution(mesh):
    return jax.shard_map(
        per_device,
        mesh=mesh,
        in_specs=(
            P(None, ("wide", "narrow")),
            P(("wide", "narrow")),
            P("wide", None, None),
            P("wide"),
            P("wide"),
            P("wide", None, None),
            P(("wide", "narrow"), None),
            P(),
            P("narrow", None),
            P(None, "narrow"),
            P(),
            P("narrow", None),
            P(),
            P(),
            P(),
        ),
        out_specs=(P(("wide", "narrow"), None), P(("wide", "narrow"))),
        check_vma=False,
    )
```

profile of v0, /device:TPU:18, one launch (start us, length us, event | category | flops | bytes accessed | tf_op | source)
XLA Modules:
  0.0 128.1 jit_solution(469522532853063279)
XLA Ops:
  7.2 0.0 copy-start
  7.2 0.0 copy-start.8
  7.2 0.0 copy-start.9
  7.2 0.0 copy-start.5
  7.2 0.0 all-gather.5.cloned.1.call-start
  7.3 0.7 all-gather.5.cloned.1.call-update
  7.9 0.0 all-gather.7.cloned.1.call-start
  8.0 0.7 all-gather.7.cloned.1.call-update
  8.7 0.8 copy.21
  9.6 0.7 reshape.113
  10.3 16.5 %all-to-all-start = ((s32[64,1,128]{2,1,0:T(1,128)}), s32[64,1,128]{2,1,0:T(1,128)S(1)}, u32[]{:S(2)}, u32[]{:S(2)}) async-start(s32[64,1,128]{2,1,0:T(1,128)} %reshape.113), calls=%async_computation | async-start | bytes 65536 | tf_op jit(solution)/shard_map/all_to_all | solution.py:45
  26.8 0.0 all-gather.9.cloned.1.call-start
  26.8 0.7 all-gather.9.cloned.1.call-update
  27.5 1.4 %fusion.32 = (s32[1]{0:T(128)}, s32[1]{0:T(128)}) fusion(s32[2]{0:T(128)} %param.21), kind=kLoop, calls=%fused_computation.59 | loop fusion | bytes 16 | tf_op jit(solution)/shard_map/slice | solution.py:33
  30.3 1.3 %convolution_convert_fusion.1 = bf16[1024,128]{1,0:T(8,128)(2,1)S(1)} fusion(bf16[2,1024,256]{2,1,0:T(8,128)(2,1)} %param.19, pred[256]{0:T(512)(128)(4,1)S(1)} %iota_compare_fusion.3, bf16[2,256,128]{2,1,0:T(8,128)(2,1)} %param.22), kind=kOutput, calls=%fused_computation.7 | convolution fusion | flops 67502080 | bytes 852224 | tf_op jit(solution)/shard_map/dot_general | solution.py:37
  31.6 0.0 copy-done.8
  31.6 0.0 copy-done.9
  31.6 0.3 convolution_convert_fusion
  31.9 0.0 copy-done.5
  31.9 0.7 fusion.31
  35.3 1.6 %all-to-all-done = s32[64,1,128]{2,1,0:T(1,128)S(1)} async-done(((s32[64,1,128]{2,1,0:T(1,128)}), s32[64,1,128]{2,1,0:T(1,128)S(1)}, u32[]{:S(2)}, u32[]{:S(2)}) %all-to-all-start) | async-done | bytes 32800 | tf_op jit(solution)/shard_map/all_to_all | solution.py:45
  36.9 0.5 broadcast.42
  37.4 0.7 reduce.4
  38.1 0.1 reshape.114
  38.2 4.9 %slice_remainder_fusion.1 = (s32[64,1,64]{2,1,0:T(1,128)S(1)}, s32[64,1,64]{2,1,0:T(1,128)S(1)}) fusion(s32[64,2,64]{2,1,0:T(2,128)S(1)} %reshape.114, s32[]{:T(128)S(6)} %select_n.37, s32[]{:T(128)S(6)} %select_n.41), kind=kLoop, calls=%fused_computation.41 | loop fusion | flops 8192 | bytes 65544 | tf_op jit(solution)/shard_map/jit(remainder)/rem | solution.py:48
  43.2 0.1 reshape.98
  43.3 0.1 reshape.102
  43.3 12.1 %gather_fusion = bf16[4096,128]{1,0:T(8,128)(2,1)S(1)} fusion(bf16[1024,128]{1,0:T(8,128)(2,1)S(1)} %convolution_convert_fusion.1, s32[4096]{0:T(1024)S(1)} %broadcast_clamp_fusion.1), kind=kCustom, calls=%fused_computation.clone | custom fusion | bytes 2113536 | tf_op jit(solution)/shard_map/jit(_take)/gather | solution.py:49
  55.5 15.0 %gather_fusion.1 = bf16[4096,128]{1,0:T(8,128)(2,1)} fusion(bf16[1024,128]{1,0:T(8,128)(2,1)S(1)} %convolution_convert_fusion, s32[4096]{0:T(1024)S(1)} %broadcast_clamp_fusion), kind=kCustom, calls=%fused_computation.1.clone | custom fusion | bytes 2113536 | tf_op jit(solution)/shard_map/jit(_take)/gather | solution.py:49
  70.5 0.0 copy-start.4
  70.5 4.0 %fusion.5 = bf16[64,1,64,128]{3,2,1,0:T(8,128)(2,1)} fusion(bf16[64,64,128]{2,1,0:T(8,128)(2,1)} %bitcast.55, bf16[64,64,128]{2,1,0:T(8,128)(2,1)S(1)} %bitcast.54, pred[64,64]{1,0:T(8,128)(4,1)S(1)} %get-tuple-element.5, pred[64,64]{1,0:T(8,128)(4,1)S(1)} %get-tuple-element.13), kind=kLoop, calls=%fused_computation.18 | loop fusion | flops 1572864 | bytes 3153920 | tf_op jit(solution)/shard_map/convert_element_type | solution.py:51
  74.6 0.0 copy-start.7
  74.6 0.0 copy-start.3
  74.6 11.3 %all-to-all-start.1 = ((bf16[64,1,64,128]{3,2,1,0:T(8,128)(2,1)}), bf16[64,1,64,128]{3,2,1,0:T(8,128)(2,1)S(1)}, u32[]{:S(2)}, u32[]{:S(2)}) async-start(bf16[64,1,64,128]{3,2,1,0:T(8,128)(2,1)} %fusion.5), calls=%async_computation.1 | async-start | bytes 2097152 | tf_op jit(solution)/shard_map/all_to_all | solution.py:52
  85.9 0.0 copy-done
  85.9 0.0 copy-done.4
  85.9 0.2 fusion.22
  86.2 11.6 %all-gather = bf16[8192]{0:T(1024)(128)(2,1)S(1)} all-gather(bf16[1024]{0:T(1024)(128)(2,1)S(1)} %multiply_convert_fusion), channel_id=2, replica_groups=mesh['wide'=64,'narrow'=8] {'narrow'}, dimensions={0}, use_global_device_ids=true | all-gather | bytes 18432 | tf_op jit(solution)/shard_map/all_gather | solution.py:61
  97.8 0.0 copy-done.7
  97.8 0.2 convolution_convert_fusion.2
  98.1 17.6 %all-to-all-done.1 = bf16[64,1,64,128]{3,2,1,0:T(8,128)(2,1)S(1)} async-done(((bf16[64,1,64,128]{3,2,1,0:T(8,128)(2,1)}), bf16[64,1,64,128]{3,2,1,0:T(8,128)(2,1)S(1)}, u32[]{:S(2)}, u32[]{:S(2)}) %all-to-all-start.1) | async-done | bytes 1048608 | tf_op jit(solution)/shard_map/all_to_all | solution.py:52
  115.7 0.0 copy-start.10
  115.7 0.0 copy-start.1
  115.7 0.2 bitcast_reduce_fusion
  115.9 0.0 all-gather.5.cloned.1.call-done
  115.9 0.0 all-gather.7.cloned.1.call-done
  115.9 0.0 copy-done.3
  116.0 2.3 %fusion.2 = bf16[64,2048]{1,0:T(8,128)(2,1)S(1)} fusion(bf16[256,2048]{1,0:T(8,128)(2,1)} %all-gather.7.cloned.1.call-done, bf16[2048,256]{1,0:T(8,128)(2,1)} %all-gather.5.cloned.1.call-done, f32[2048]{0:T(1024)S(1)} %copy-done.3, bf16[64,1024]{1,0:T(8,128)(2,1)S(1)} %copy_bitcast_fusion, bf16[64,1024]{1,0:T(8,128)(2,1)S(1)} %convolution_convert_fusion.2), kind=kOutput, calls=%fused_computation.5 | convolution fusion | flops 135806976 | bytes 2629632 | tf_op jit(solution)/shard_map/dot_general | solution.py:80
  118.3 0.0 copy-start.2
  118.3 0.0 copy-start.6
  118.3 0.0 copy-done.10
  118.3 0.3 convolution_bitcast_fusion.1
  118.7 0.0 all-gather.9.cloned.1.call-done
  118.7 0.0 copy-done.1
  118.7 2.2 %convolution_maximum_fusion.1 = f32[64,256]{1,0:T(8,128)S(1)} fusion(bf16[512,256]{1,0:T(8,128)(2,1)S(1)} %copy-done.1, bf16[2048,512]{1,0:T(8,128)(2,1)} %all-gather.9.cloned.1.call-done, bf16[64,1024]{1,0:T(8,128)(2,1)S(1)} %copy_bitcast_fusion, bf16[64,1024]{1,0:T(8,128)(2,1)S(1)} %convolution_convert_fusion.2), kind=kOutput, calls=%fused_computation.11 | convolution fusion | flops 151601152 | bytes 2686976 | tf_op jit(solution)/shard_map/dot_general | solution.py:87
  120.9 0.0 copy-done.6
  120.9 0.7 fusion.4
  121.6 0.0 copy-done.2
  (8 shorter events, 0.1 us)
Async XLA Ops:
  7.2 78.8 %copy-start = (bf16[512,1024]{1,0:T(8,128)(2,1)S(1)}, bf16[512,1024]{1,0:T(8,128)(2,1)}, u32[]{:S(2)}) copy-start(bf16[512,1024]{1,0:T(8,128)(2,1)} %param.24) | copy-start | bytes 3145732
  7.2 24.4 %copy-start.8 = (bf16[2,1024,256]{2,1,0:T(8,128)(2,1)S(1)}, bf16[2,1024,256]{2,1,0:T(8,128)(2,1)}, u32[]{:S(2)}) copy-start(bf16[2,1024,256]{2,1,0:T(8,128)(2,1)} %param.19) | copy-start | bytes 3145732
  7.2 24.4 %copy-start.9 = (bf16[2,256,128]{2,1,0:T(8,128)(2,1)S(1)}, bf16[2,256,128]{2,1,0:T(8,128)(2,1)}, u32[]{:S(2)}) copy-start(bf16[2,256,128]{2,1,0:T(8,128)(2,1)} %param.22) | copy-start | bytes 393220
  7.2 24.7 %copy-start.5 = (s32[2]{0:T(128)S(1)}, s32[2]{0:T(128)}, u32[]{:S(2)}) copy-start(s32[2]{0:T(128)} %param.20) | copy-start | bytes 28
  7.2 108.7 %all-gather.5.cloned.1.call-start = ((), (), s32[]{:S(2)}) async-start(), calls=%async_computation.2 | async-start | bytes 1179648 | tf_op jit(solution)/shard_map/all_gather | solution.py:70
  7.9 108.0 %all-gather.7.cloned.1.call-start = ((), (), s32[]{:S(2)}) async-start(), calls=%async_computation.3 | async-start | bytes 1179648 | tf_op jit(solution)/shard_map/all_gather | solution.py:82
  10.3 26.6 %all-to-all-start = ((s32[64,1,128]{2,1,0:T(1,128)}), s32[64,1,128]{2,1,0:T(1,128)S(1)}, u32[]{:S(2)}, u32[]{:S(2)}) async-start(s32[64,1,128]{2,1,0:T(1,128)} %reshape.113), calls=%async_computation | async-start | bytes 65536 | tf_op jit(solution)/shard_map/all_to_all | solution.py:45
  26.8 91.9 %all-gather.9.cloned.1.call-start = ((), (), s32[]{:S(2)}) async-start(), calls=%async_computation.4 | async-start | bytes 2359296 | tf_op jit(solution)/shard_map/all_gather | solution.py:75
  70.5 15.4 %copy-start.4 = (bf16[1,512]{1,0:T(2,128)(2,1)S(1)}, bf16[1,512]{1,0:T(2,128)(2,1)}, u32[]{:S(2)}) copy-start(bf16[1,512]{1,0:T(2,128)(2,1)} %param.23) | copy-start | bytes 3076
  74.6 23.3 %copy-start.7 = (s32[64]{0:T(128)S(1)}, s32[64]{0:T(128)}, u32[]{:S(2)}) copy-start(s32[64]{0:T(128)} %param.18) | copy-start | bytes 772
  74.6 41.4 %copy-start.3 = (f32[2048]{0:T(1024)S(1)}, f32[2048]{0:T(1024)}, u32[]{:S(2)}) copy-start(f32[2048]{0:T(1024)} %param.27) | copy-start | bytes 24580
  74.6 41.1 %all-to-all-start.1 = ((bf16[64,1,64,128]{3,2,1,0:T(8,128)(2,1)}), bf16[64,1,64,128]{3,2,1,0:T(8,128)(2,1)S(1)}, u32[]{:S(2)}, u32[]{:S(2)}) async-start(bf16[64,1,64,128]{3,2,1,0:T(8,128)(2,1)} %fusion.5), calls=%async_computation.1 | async-start | bytes 2097152 | tf_op jit(solution)/shard_map/all_to_all | solution.py:52
  115.7 2.6 %copy-start.10 = (f32[2048]{0:T(1024)S(1)}, f32[2048]{0:T(1024)}, u32[]{:S(2)}) copy-start(f32[2048]{0:T(1024)} %param.30) | copy-start | bytes 24580
  115.7 3.0 %copy-start.1 = (bf16[512,256]{1,0:T(8,128)(2,1)S(1)}, bf16[512,256]{1,0:T(8,128)(2,1)}, u32[]{:S(2)}) copy-start(bf16[512,256]{1,0:T(8,128)(2,1)} %param.29) | copy-start | bytes 786436
  118.3 3.3 %copy-start.2 = (bf16[64,2048]{1,0:T(8,128)(2,1)}, bf16[64,2048]{1,0:T(8,128)(2,1)S(1)}, u32[]{:S(2)}) copy-start(bf16[64,2048]{1,0:T(8,128)(2,1)S(1)} %fusion.2) | copy-start | bytes 786436
  118.3 2.6 %copy-start.6 = (f32[256]{0:T(256)S(1)}, f32[256]{0:T(256)}, u32[]{:S(2)}) copy-start(f32[256]{0:T(256)} %param.31) | copy-start | bytes 3076
Sparse Core Ops, SparseCore 0:
  10.2 31.6 all-gather.4
  44.0 29.4 all-gather.6
  75.7 30.8 all-gather.8
where the time goes:
time: 129 us; the launch traced here: 128 us
  local copies, waits for them, and re-layouts  31.7 us (25%)
  starting transfers between devices  27.9 us (22%)
  waiting for transfers between devices  21.3 us (17%)
  between operations  18 us (14%)
  blocking collectives  11.6 us (9%)
  other arithmetic  9.9 us (8%)
  matrix products  7.65 us (6%)
    gather x2, local copies, waits for them, and re-layouts, per_device(): results.append(jnp.take(projected[t], index, axis=0))  27.2 us
    all_to_all x1, waiting for transfers between devices, per_device(): lax.all_to_all(pooled, 'wide', split_axis=0, concat_axis=0, tiled=True)  17.6 us
    all_to_all x1, starting transfers between devices, per_device(): lax.all_to_all(feature_ids, 'wide', split_axis=0, concat_axis=0, tiled=True)  16.5 us
    all_gather x1, blocking collectives, per_device(): users = lax.all_gather(mine, 'narrow', axis=0, tiled=True)  11.6 us
    all_to_all x1, starting transfers between devices, per_device(): lax.all_to_all(pooled, 'wide', split_axis=0, concat_axis=0, tiled=True)  11.3 us
    rem x1, other arithmetic, per_device(): index = jnp.remainder(received[:, t, :], table_rows[t])  4.92 us
    convert_element_type x1, other arithmetic, per_device(): jnp.sum(stacked, axis=1, keepdims=True, dtype=jnp.float32)  4.02 us
  transfers between devices with their start and end apart: 5, of which 2 were waited for; matrix products, arithmetic and copies ran while one was open for 36% of the time, Pallas kernels for 0%

commit v1 on v0

--- a/solution.py
+++ b/solution.py
@@ -58,7 +58,9 @@
     mine = jax.nn.silu(jnp.dot(user_dense, user_weight, preferred_element_type=jnp.float32)).astype(
         jnp.bfloat16
     )
-    users = lax.all_gather(mine, "narrow", axis=0, tiled=True)
+    users = jnp.concatenate(
+        lax.all_to_all(jnp.stack([mine] * lax.axis_size("narrow")), "narrow", 0, 0), axis=0
+    )
     req_count = users.shape[0]
     selector = (cand_request[:, None] == jnp.arange(req_count, dtype=jnp.int32)[None, :]).astype(
         jnp.bfloat16

time: 129 us -> 136 us (1.054)
  blocking collectives: 11.6 us -> 0 us
  waiting for transfers between devices: 21.3 us -> 32.5 us
  starting transfers between devices: 27.9 us -> 34.3 us
    all_to_all x1, waiting for transfers between devices: 17.6 us -> 30.4 us  [per_device(): lax.all_to_all(pooled, 'wide', split_axis=0, concat_axis=0, tiled=True)]
    all_gather x1 -> x0, blocking collectives: 11.6 us -> none  [per_device(): users = lax.all_gather(mine, 'narrow', axis=0, tiled=True)]
    all_to_all x0 -> x1, starting transfers between devices: none -> 4.83 us  [per_device(): lax.all_to_all(jnp.stack([mine] * lax.axis_size('narrow')), 'narrow', 0, 0)]
    all_to_all x1, waiting for transfers between devices: 1.58 us -> 0.01 us  [per_device(): lax.all_to_all(feature_ids, 'wide', split_axis=0, concat_axis=0, tiled=True)]
    all_to_all x1, starting transfers between devices: 11.3 us -> 12.9 us  [per_device(): lax.all_to_all(pooled, 'wide', split_axis=0, concat_axis=0, tiled=True)]
  transfers between devices with their start and end apart: 5 -> 6, of which waited for: 2 -> 1; matrix products, arithmetic and copies ran while one was open for 36% -> 35% of each run, Pallas kernels for 0% -> 0%
where the time goes in v1:
time: 136 us
  starting transfers between devices  34.3 us (25%)
  local copies, waits for them, and re-layouts  32.6 us (24%)
  waiting for transfers between devices  32.5 us (24%)
  between operations  18 us (13%)
  other arithmetic  10.6 us (8%)
  matrix products  7.65 us (6%)
    all_to_all x1, waiting for transfers between devices, per_device(): lax.all_to_all(pooled, 'wide', split_axis=0, concat_axis=0, tiled=True)  30.4 us
    gather x2, local copies, waits for them, and re-layouts, per_device(): results.append(jnp.take(projected[t], index, axis=0))  27 us
    all_to_all x1, starting transfers between devices, per_device(): lax.all_to_all(feature_ids, 'wide', split_axis=0, concat_axis=0, tiled=True)  16.5 us
    all_to_all x1, starting transfers between devices, per_device(): lax.all_to_all(pooled, 'wide', split_axis=0, concat_axis=0, tiled=True)  12.9 us
    rem x1, other arithmetic, per_device(): index = jnp.remainder(received[:, t, :], table_rows[t])  4.92 us
    all_to_all x1, starting transfers between devices, per_device(): lax.all_to_all(jnp.stack([mine] * lax.axis_size('narrow')), 'narrow', 0, 0)  4.83 us
    convert_element_type x1, other arithmetic, per_device(): jnp.sum(stacked, axis=1, keepdims=True, dtype=jnp.float32)  4.03 us
  transfers between devices with their start and end apart: 6, of which 1 were waited for; matrix products, arithmetic and copies ran while one was open for 35% of the time, Pallas kernels for 0%

profile of v1, /device:TPU:18, one launch (start us, length us, event | category | flops | bytes accessed | tf_op | source)
XLA Modules:
  0.0 135.7 jit_solution(9516285231155779339)
XLA Ops:
  7.2 0.0 copy-start
  7.2 0.0 copy-start.8
  7.2 0.0 copy-start.9
  7.2 0.0 copy-start.4
  7.2 0.0 all-gather.4.cloned.1.call-start
  7.3 0.7 all-gather.4.cloned.1.call-update
  7.9 0.0 all-gather.6.cloned.1.call-start
  8.0 0.7 all-gather.6.cloned.1.call-update
  8.7 0.8 copy.21
  9.6 0.0 copy-start.5
  9.6 0.7 reshape.119
  10.3 16.5 %all-to-all-start.1 = ((s32[64,1,128]{2,1,0:T(1,128)}), s32[64,1,128]{2,1,0:T(1,128)S(1)}, u32[]{:S(2)}, u32[]{:S(2)}) async-start(s32[64,1,128]{2,1,0:T(1,128)} %reshape.119), calls=%async_computation.1 | async-start | bytes 65536 | tf_op jit(solution)/shard_map/all_to_all | solution.py:45
  26.8 0.0 all-gather.8.cloned.1.call-start
  26.8 0.7 all-gather.8.cloned.1.call-update
  27.5 1.4 %fusion.34 = (s32[1]{0:T(128)}, s32[1]{0:T(128)}) fusion(s32[2]{0:T(128)} %param.21), kind=kLoop, calls=%fused_computation.61 | loop fusion | bytes 16 | tf_op jit(solution)/shard_map/slice | solution.py:33
  30.2 1.3 convolution_convert_fusion.1
  31.6 0.0 copy-done.8
  31.6 0.0 copy-done.9
  31.6 0.3 convolution_convert_fusion
  31.9 0.0 copy-done
  31.9 0.0 copy-done.4
  31.9 0.2 fusion.24
  32.2 0.0 copy-done.5
  32.2 0.7 fusion.33
  35.5 0.5 broadcast.45
  36.0 0.7 reduce.5
  36.8 0.6 reshape.121
  37.4 0.0 all-to-all-done.1
  37.4 4.8 %all-to-all-start = ((bf16[8,2,512]{2,1,0:T(2,128)(2,1)}), bf16[8,2,512]{2,1,0:T(2,128)(2,1)S(1)}, u32[]{:S(2)}, u32[]{:S(2)}) async-start(bf16[8,2,512]{2,1,0:T(2,128)(2,1)} %reshape.121), calls=%async_computation | async-start | bytes 32768 | tf_op jit(solution)/shard_map/all_to_all | solution.py:62
  42.2 0.5 broadcast.44
  42.7 0.7 reduce.4
  43.5 0.1 reshape.120
  43.6 4.9 %slice_remainder_fusion.1 = (s32[64,1,64]{2,1,0:T(1,128)S(1)}, s32[64,1,64]{2,1,0:T(1,128)S(1)}) fusion(s32[64,2,64]{2,1,0:T(2,128)S(1)} %reshape.120, s32[]{:T(128)S(6)} %select_n.37, s32[]{:T(128)S(6)} %select_n.41), kind=kLoop, calls=%fused_computation.41 | loop fusion | flops 8192 | bytes 65544 | tf_op jit(solution)/shard_map/jit(remainder)/rem | solution.py:48
  48.5 0.1 reshape.104
  48.6 0.1 reshape.108
  48.7 12.1 %gather_fusion = bf16[4096,128]{1,0:T(8,128)(2,1)S(1)} fusion(bf16[1024,128]{1,0:T(8,128)(2,1)S(1)} %convolution_convert_fusion.1, s32[4096]{0:T(1024)S(1)} %broadcast_clamp_fusion.1), kind=kCustom, calls=%fused_computation.clone | custom fusion | bytes 2113536 | tf_op jit(solution)/shard_map/jit(_take)/gather | solution.py:49
  60.9 14.9 %gather_fusion.1 = bf16[4096,128]{1,0:T(8,128)(2,1)} fusion(bf16[1024,128]{1,0:T(8,128)(2,1)S(1)} %convolution_convert_fusion, s32[4096]{0:T(1024)S(1)} %broadcast_clamp_fusion), kind=kCustom, calls=%fused_computation.1.clone | custom fusion | bytes 2113536 | tf_op jit(solution)/shard_map/jit(_take)/gather | solution.py:49
  75.7 0.0 copy-start.7
  75.7 4.0 %fusion.5 = bf16[64,1,64,128]{3,2,1,0:T(8,128)(2,1)} fusion(bf16[64,64,128]{2,1,0:T(8,128)(2,1)} %bitcast.57, bf16[64,64,128]{2,1,0:T(8,128)(2,1)S(1)} %bitcast.56, pred[64,64]{1,0:T(8,128)(4,1)S(1)} %get-tuple-element.5, pred[64,64]{1,0:T(8,128)(4,1)S(1)} %get-tuple-element.13), kind=kLoop, calls=%fused_computation.18 | loop fusion | flops 1572864 | bytes 3153920 | tf_op jit(solution)/shard_map/convert_element_type | solution.py:51
  79.8 0.0 copy-start.3
  79.8 0.0 all-to-all-done
  79.8 12.9 %all-to-all-start.2 = ((bf16[64,1,64,128]{3,2,1,0:T(8,128)(2,1)}), bf16[64,1,64,128]{3,2,1,0:T(8,128)(2,1)S(1)}, u32[]{:S(2)}, u32[]{:S(2)}) async-start(bf16[64,1,64,128]{3,2,1,0:T(8,128)(2,1)} %fusion.5), calls=%async_computation.2 | async-start | bytes 2097152 | tf_op jit(solution)/shard_map/all_to_all | solution.py:52
  92.7 0.0 copy-done.7
  92.7 0.2 convolution_convert_fusion.2
  92.9 30.4 %all-to-all-done.2 = bf16[64,1,64,128]{3,2,1,0:T(8,128)(2,1)S(1)} async-done(((bf16[64,1,64,128]{3,2,1,0:T(8,128)(2,1)}), bf16[64,1,64,128]{3,2,1,0:T(8,128)(2,1)S(1)}, u32[]{:S(2)}, u32[]{:S(2)}) %all-to-all-start.2) | async-done | bytes 1048608 | tf_op jit(solution)/shard_map/all_to_all | solution.py:52
  123.3 0.0 copy-start.10
  123.3 0.0 copy-start.1
  123.3 0.2 bitcast_reduce_fusion
  123.5 0.0 all-gather.4.cloned.1.call-done
  123.6 0.0 all-gather.6.cloned.1.call-done
  123.6 0.0 copy-done.3
  123.6 2.3 %fusion.2 = bf16[64,2048]{1,0:T(8,128)(2,1)S(1)} fusion(bf16[256,2048]{1,0:T(8,128)(2,1)} %all-gather.6.cloned.1.call-done, bf16[2048,256]{1,0:T(8,128)(2,1)} %all-gather.4.cloned.1.call-done, f32[2048]{0:T(1024)S(1)} %copy-done.3, bf16[64,1024]{1,0:T(8,128)(2,1)S(1)} %copy_bitcast_fusion, bf16[64,1024]{1,0:T(8,128)(2,1)S(1)} %convolution_convert_fusion.2), kind=kOutput, calls=%fused_computation.5 | convolution fusion | flops 135806976 | bytes 2629632 | tf_op jit(solution)/shard_map/dot_general | solution.py:82
  125.9 0.0 copy-start.2
  126.0 0.0 copy-start.6
  126.0 0.0 copy-done.10
  126.0 0.3 convolution_bitcast_fusion.1
  126.3 0.0 all-gather.8.cloned.1.call-done
  126.3 0.0 copy-done.1
  126.3 2.2 %convolution_maximum_fusion.1 = f32[64,256]{1,0:T(8,128)S(1)} fusion(bf16[512,256]{1,0:T(8,128)(2,1)S(1)} %copy-done.1, bf16[2048,512]{1,0:T(8,128)(2,1)} %all-gather.8.cloned.1.call-done, bf16[64,1024]{1,0:T(8,128)(2,1)S(1)} %copy_bitcast_fusion, bf16[64,1024]{1,0:T(8,128)(2,1)S(1)} %convolution_convert_fusion.2), kind=kOutput, calls=%fused_computation.11 | convolution fusion | flops 151601152 | bytes 2686976 | tf_op jit(solution)/shard_map/dot_general | solution.py:89
  128.5 0.0 copy-done.6
  128.5 0.7 fusion.4
  129.2 0.0 copy-done.2
  (9 shorter events, 0.1 us)
Async XLA Ops:
  7.2 24.7 %copy-start = (bf16[512,1024]{1,0:T(8,128)(2,1)S(1)}, bf16[512,1024]{1,0:T(8,128)(2,1)}, u32[]{:S(2)}) copy-start(bf16[512,1024]{1,0:T(8,128)(2,1)} %param.24) | copy-start | bytes 3145732
  7.2 24.4 %copy-start.8 = (bf16[2,1024,256]{2,1,0:T(8,128)(2,1)S(1)}, bf16[2,1024,256]{2,1,0:T(8,128)(2,1)}, u32[]{:S(2)}) copy-start(bf16[2,1024,256]{2,1,0:T(8,128)(2,1)} %param.19) | copy-start | bytes 3145732
  7.2 24.4 %copy-start.9 = (bf16[2,256,128]{2,1,0:T(8,128)(2,1)S(1)}, bf16[2,256,128]{2,1,0:T(8,128)(2,1)}, u32[]{:S(2)}) copy-start(bf16[2,256,128]{2,1,0:T(8,128)(2,1)} %param.22) | copy-start | bytes 393220
  7.2 24.7 %copy-start.4 = (bf16[1,512]{1,0:T(2,128)(2,1)S(1)}, bf16[1,512]{1,0:T(2,128)(2,1)}, u32[]{:S(2)}) copy-start(bf16[1,512]{1,0:T(2,128)(2,1)} %param.23) | copy-start | bytes 3076
  7.2 116.3 %all-gather.4.cloned.1.call-start = ((), (), s32[]{:S(2)}) async-start(), calls=%async_computation.3 | async-start | bytes 1179648 | tf_op jit(solution)/shard_map/all_gather | solution.py:72
  7.9 115.6 %all-gather.6.cloned.1.call-start = ((), (), s32[]{:S(2)}) async-start(), calls=%async_computation.4 | async-start | bytes 1179648 | tf_op jit(solution)/shard_map/all_gather | solution.py:84
  9.6 22.6 %copy-start.5 = (s32[2]{0:T(128)S(1)}, s32[2]{0:T(128)}, u32[]{:S(2)}) copy-start(s32[2]{0:T(128)} %param.20) | copy-start | bytes 28
  10.3 27.1 %all-to-all-start.1 = ((s32[64,1,128]{2,1,0:T(1,128)}), s32[64,1,128]{2,1,0:T(1,128)S(1)}, u32[]{:S(2)}, u32[]{:S(2)}) async-start(s32[64,1,128]{2,1,0:T(1,128)} %reshape.119), calls=%async_computation.1 | async-start | bytes 65536 | tf_op jit(solution)/shard_map/all_to_all | solution.py:45
  26.8 99.5 %all-gather.8.cloned.1.call-start = ((), (), s32[]{:S(2)}) async-start(), calls=%async_computation.5 | async-start | bytes 2359296 | tf_op jit(solution)/shard_map/all_gather | solution.py:77
  37.4 42.4 %all-to-all-start = ((bf16[8,2,512]{2,1,0:T(2,128)(2,1)}), bf16[8,2,512]{2,1,0:T(2,128)(2,1)S(1)}, u32[]{:S(2)}, u32[]{:S(2)}) async-start(bf16[8,2,512]{2,1,0:T(2,128)(2,1)} %reshape.121), calls=%async_computation | async-start | bytes 32768 | tf_op jit(solution)/shard_map/all_to_all | solution.py:62
  75.7 17.0 %copy-start.7 = (s32[64]{0:T(128)S(1)}, s32[64]{0:T(128)}, u32[]{:S(2)}) copy-start(s32[64]{0:T(128)} %param.18) | copy-start | bytes 772
  79.8 43.8 %copy-start.3 = (f32[2048]{0:T(1024)S(1)}, f32[2048]{0:T(1024)}, u32[]{:S(2)}) copy-start(f32[2048]{0:T(1024)} %param.27) | copy-start | bytes 24580
  79.8 43.5 %all-to-all-start.2 = ((bf16[64,1,64,128]{3,2,1,0:T(8,128)(2,1)}), bf16[64,1,64,128]{3,2,1,0:T(8,128)(2,1)S(1)}, u32[]{:S(2)}, u32[]{:S(2)}) async-start(bf16[64,1,64,128]{3,2,1,0:T(8,128)(2,1)} %fusion.5), calls=%async_computation.2 | async-start | bytes 2097152 | tf_op jit(solution)/shard_map/all_to_all | solution.py:52
  123.3 2.6 %copy-start.10 = (f32[2048]{0:T(1024)S(1)}, f32[2048]{0:T(1024)}, u32[]{:S(2)}) copy-start(f32[2048]{0:T(1024)} %param.30) | copy-start | bytes 24580
  123.3 3.0 %copy-start.1 = (bf16[512,256]{1,0:T(8,128)(2,1)S(1)}, bf16[512,256]{1,0:T(8,128)(2,1)}, u32[]{:S(2)}) copy-start(bf16[512,256]{1,0:T(8,128)(2,1)} %param.29) | copy-start | bytes 786436
  125.9 3.3 %copy-start.2 = (bf16[64,2048]{1,0:T(8,128)(2,1)}, bf16[64,2048]{1,0:T(8,128)(2,1)S(1)}, u32[]{:S(2)}) copy-start(bf16[64,2048]{1,0:T(8,128)(2,1)S(1)} %fusion.2) | copy-start | bytes 786436
  126.0 2.6 %copy-start.6 = (f32[256]{0:T(256)S(1)}, f32[256]{0:T(256)}, u32[]{:S(2)}) copy-start(f32[256]{0:T(256)} %param.31) | copy-start | bytes 3076
Sparse Core Ops, SparseCore 0:
  10.2 31.6 all-gather.3
  44.0 29.5 all-gather.5
  75.7 30.8 all-gather.7
